TPU v7x, 128 devices: a whole 4x4x4 slice. The times are simulated.
128 devices in a mesh: dp: 32 (over y, z, core), sp: 4 (over x).
Axes of the slice: x: 4, y: 4, z: 4, core: 2. Of those that a mesh axis runs over, the one named last changes fastest.
Arguments:
- queries: bfloat16 [32, 512, 4096], P('dp', 'sp'), may hold values from -30 to 30
- rotated_span_keys: bfloat16 [32, 512, 512], P('dp', 'sp'), may hold values from -6 to 6
- span_value_heads: bfloat16 [32, 512, 512], P('dp', 'sp'), may hold values from -6 to 6
- cache_keys: bfloat16 [32, 4, 8192, 128], P('dp', 'sp'), may hold values from -6 to 6
- cached_prefix_values: bfloat16 [32, 4, 8192, 128], P('dp', 'sp'), may hold values from -6 to 6
- out_weight: bfloat16 [4096, 8192], P('sp', 'dp'), may hold values from -0.09375 to 0.09375
- prefix_lengths: int32 [32], replicated, may hold values from 2 to 8192, as said below
- valid_lengths: int32 [32], replicated, may hold values from 256 to 512, as said below
Outputs:
- output: bfloat16 [32, 512, 8192], P('dp', 'sp')
Inputs may be any that keep to these rules, and one draw needn't show every extreme that they name: Trajectory b's live cache slots are 0 to prefix_lengths[b] - 1; some trajectory has exactly 8192. Span positions from valid_lengths[b] on are padding; some trajectory has exactly 512.
All inputs are finite; a program needn't handle non-finite values.
Results may differ from a plain program's by a relative error of at most 0.013.
Values may be sent and summed in bfloat16 or wider, within the bound.
No kernel may reach another device: no remote copies, remote signals or barrier semaphores. Data moves between devices by JAX's collectives and lax.ppermute only.
A program may use at most 128 MiB of HBM per device.

v0:
```python
import math

import jax
import jax.numpy as jnp
from jax import lax
from jax.sharding import PartitionSpec as P

NEGATIVE = -1e30


def block_update(carried, query_rows, key_block, value_block, usable, score_scale):
    running_max, running_sum, weighted = carried
    scores = (
        jnp.einsum("grd,gkd->grk", query_rows, key_block, preferred_element_type=jnp.float32)
        * score_scale
    )
    scores = jnp.where(usable, scores, NEGATIVE)
    highest = jnp.maximum(running_max, jnp.max(scores, axis=-1))
    weights = jnp.exp(scores - highest[..., None])
    rescale = jnp.exp(running_max - highest)
    running_sum = running_sum * rescale + jnp.sum(weights, axis=-1)
    weighted = weighted * rescale[..., None] + jnp.einsum(
        "grk,gkd->grd",
        weights.astype(jnp.bfloat16),
        value_block,
        preferred_element_type=jnp.float32,
    )
    return (highest, running_sum, weighted)


def prefix_pass(
    carried, query_rows, prefix_keys, prefix_values, first_position, length, score_scale
):
    stored = prefix_keys.shape[1]
    block_len = math.gcd(512, stored)
    live_count = jnp.clip(length - first_position, 0, stored)
    block_count = (live_count + block_len - 1) // block_len

    def visit(block_index, running):
        key_block = lax.dynamic_slice_in_dim(prefix_keys, block_index * block_len, block_len, 1)
        value_block = lax.dynamic_slice_in_dim(prefix_values, block_index * block_len, block_len, 1)
        position = block_index * block_len + jnp.arange(block_len, dtype=jnp.int32)
        usable = (position < live_count)[None, None, :]
        return block_update(running, query_rows, key_block, value_block, usable, score_scale)

    return lax.fori_loop(jnp.int32(0), block_count, visit, carried)


def span_pass(carried, query_rows, fresh_keys, fresh_values, query_position, score_scale):
    span_len = fresh_keys.shape[1]
    block_len = math.gcd(512, span_len)
    key_position = 0 + jnp.arange(block_len, dtype=jnp.int32)
    usable = (key_position[None, :] <= query_position[:, None])[None]
    carried = block_update(carried, query_rows, fresh_keys, fresh_values, usable, score_scale)
    return carried


def local(
    queries,
    rotated_span_keys,
    span_value_heads,
    cache_keys,
    cached_prefix_values,
    out_weight,
    prefix_lengths,
    valid_lengths,
):
    seq_parts = lax.axis_size("sp")
    gathered_q, gathered_k, gathered_v = (
        lax.all_to_all(queries, "sp", split_axis=2, concat_axis=1, tiled=True),
        lax.all_to_all(rotated_span_keys, "sp", split_axis=2, concat_axis=1, tiled=True),
        lax.all_to_all(span_value_heads, "sp", split_axis=2, concat_axis=1, tiled=True),
    )
    span_len = gathered_q.shape[1]
    kv_groups = cache_keys.shape[1]
    head_dim = cache_keys.shape[3]
    group_width = gathered_q.shape[2] // (kv_groups * head_dim)
    row_count = group_width * span_len
    query_rows = (
        gathered_q[0].reshape(span_len, kv_groups, group_width, head_dim).transpose(1, 2, 0, 3)
    )
    query_rows = query_rows.reshape(kv_groups, row_count, head_dim)
    fresh_keys = gathered_k[0].reshape(span_len, kv_groups, head_dim).transpose(1, 0, 2)
    fresh_values = gathered_v[0].reshape(span_len, kv_groups, head_dim).transpose(1, 0, 2)
    score_scale = 1.0 / math.sqrt(head_dim)
    query_position = jnp.arange(row_count, dtype=jnp.int32) % span_len
    device_row = lax.axis_index("dp")
    own_prefix = lax.dynamic_index_in_dim(prefix_lengths, device_row, 0, keepdims=False)
    own_valid = lax.dynamic_index_in_dim(valid_lengths, device_row, 0, keepdims=False)
    initial = (
        jnp.full((kv_groups, row_count), NEGATIVE, jnp.float32),
        jnp.zeros((kv_groups, row_count), jnp.float32),
        jnp.zeros((kv_groups, row_count, head_dim), jnp.float32),
    )
    own_keys = cache_keys[0]
    own_values = cached_prefix_values[0]
    carried = prefix_pass(initial, query_rows, own_keys, own_values, 0, own_prefix, score_scale)
    carried = span_pass(carried, query_rows, fresh_keys, fresh_values, query_position, score_scale)
    normalized = carried[2] / carried[1][..., None]
    attended = normalized.reshape(kv_groups, group_width, span_len, head_dim).transpose(2, 0, 1, 3)
    attended = attended.reshape(span_len, kv_groups * group_width * head_dim).astype(jnp.bfloat16)
    rows_mine = span_len // seq_parts
    terms = jnp.dot(
        attended,
        lax.all_gather(out_weight, "dp", axis=1, tiled=True),
        preferred_element_type=jnp.float32,
    )
    projected = lax.psum_scatter(terms.astype(jnp.bfloat16), "sp", scatter_dimension=0, tiled=True)
    token_index = lax.axis_index("sp") * rows_mine + jnp.arange(rows_mine, dtype=jnp.int32)
    keep_rows = token_index < own_valid
    result = jnp.where(keep_rows[:, None], projected, jnp.zeros_like(projected))
    return result[None]


def solution(mesh):
    in_specs = (
        P("dp", "sp", None),
        P("dp", "sp", None),
        P("dp", "sp", None),
        P("dp", "sp", None, None),
        P("dp", "sp", None, None),
        P("sp", "dp"),
        P(),
        P(),
    )
    out_specs = P("dp", "sp", None)
    return jax.shard_map(local, mesh=mesh, in_specs=in_specs, out_specs=out_specs, check_vma=False)
```

profile of v0, /device:TPU:1, one launch (start us, length us, event | category | flops | bytes accessed | tf_op | source)
XLA Modules:
  0.0 331.7 jit_solution(14578913971116587080)
XLA Ops:
  6.5 0.7 all-gather.2.cloned.1.call-update
  7.3 1.1 copy.32
  8.3 0.6 broadcast.71
  8.9 1.4 reduce.12
  10.4 0.7 reshape.99
  11.1 4.8 %all-to-all-start.1 = ((bf16[4,2,8192]{2,1,0:T(2,128)(2,1)}), bf16[4,2,8192]{2,1,0:T(2,128)(2,1)S(1)}, u32[]{:S(2)}, u32[]{:S(2)}) async-start(bf16[4,2,8192]{2,1,0:T(2,128)(2,1)} %reshape.99), calls=%async_computation.1 | async-start | bytes 262144 | tf_op jit(solution)/shard_map/all_to_all | solution.py:71
  15.9 1.1 copy.34
  17.0 1.5 reduce.10
  18.4 0.7 reshape.95
  19.1 1.6 all-to-all-done.1
  20.7 3.3 %all-to-all-start.2 = ((bf16[4,2,8192]{2,1,0:T(2,128)(2,1)}), bf16[4,2,8192]{2,1,0:T(2,128)(2,1)S(1)}, u32[]{:S(2)}, u32[]{:S(2)}) async-start(bf16[4,2,8192]{2,1,0:T(2,128)(2,1)} %reshape.95), calls=%async_computation.2 | async-start | bytes 262144 | tf_op jit(solution)/shard_map/all_to_all | solution.py:72
  24.1 5.0 %copy.28 = bf16[1,128,4096]{1,0,2:T(2,128)(2,1)S(1)} copy(bf16[1,128,4096]{2,1,0:T(8,128)(2,1)} %param.10) | data formatting | bytes 2097152 | tf_op args[0]
  29.1 22.4 %reduce.11 = bf16[4096,128]{1,0:T(8,128)(2,1)S(1)} reduce(bf16[4096,1,128]{2,1,0:T(2,128)(2,1)S(1)} %bitcast.95, bf16[]{:T(256)} %broadcast.71), dimensions={1}, to_apply=%bitcast.63.reduce_sub_computation | reduce | bytes 2097154
  51.6 1.7 reshape.97
  53.2 4.2 %all-to-all-start = ((bf16[4,2,65536]{2,1,0:T(2,128)(2,1)}), bf16[4,2,65536]{2,1,0:T(2,128)(2,1)S(1)}, u32[]{:S(2)}, u32[]{:S(2)}) async-start(bf16[4,2,65536]{2,1,0:T(2,128)(2,1)} %reshape.97), calls=%async_computation | async-start | bytes 2097152 | tf_op jit(solution)/shard_map/all_to_all | solution.py:70
  57.4 0.6 dynamic_slice.14
  58.6 0.1 reshape.100
  58.7 0.1 copy.33
  59.0 0.1 copy.35
  59.2 10.5 %all-to-all-done = bf16[4,2,65536]{2,1,0:T(2,128)(2,1)S(1)} async-done(((bf16[4,2,65536]{2,1,0:T(2,128)(2,1)}), bf16[4,2,65536]{2,1,0:T(2,128)(2,1)S(1)}, u32[]{:S(2)}, u32[]{:S(2)}) %all-to-all-start) | async-done | bytes 1048608 | tf_op jit(solution)/shard_map/all_to_all | solution.py:70
  69.7 0.9 reshape.98
  70.7 0.1 copy.37
  70.8 0.5 copy.29
  71.4 0.3 copy.40
  71.6 0.1 copy.30
  71.8 4.8 %fusion.28 = (f32[4096]{0:T(1024)S(1)}, f32[4096,512]{0,1:T(8,128)}) fusion(bf16[4096,128]{1,0:T(8,128)(2,1)S(1)} %bitcast.92, bf16[512,128]{1,0:T(8,128)(2,1)S(1)} %bitcast.116, s32[4096]{0:T(1024)S(1)} %add_select_fusion), kind=kOutput, calls=%fused_computation.43 | convolution fusion | flops 545255424 | bytes 9601024 | tf_op jit(solution)/shard_map/grd,gkd->grk/dot_general | solution.py:14
  76.6 0.1 broadcast_in_dim.52
  76.7 79.7 %while.14 = (s32[]{:T(128)}, f32[1,4096]{1,0:T(1,128)S(1)}, f32[1,4096]{1,0:T(1,128)S(1)}, f32[1,4096,128]{2,1,0:T(8,128)S(1)}, s32[]{:T(128)}, /*index=5*/s32[]...) while((s32[]{:T(128)}, f32[1,4096]{1,0:T(1,128)S(1)}, ...), condition=%wide.region_3.4_spmd, body=%wide.region_0.3_spmd.sunk | while | flops 1097868288 | bytes 30935228 | solution.py:46
  76.9 2.3 fusion.41
  79.3 2.1 fusion.42
  81.4 4.3 %fusion.43 = f32[1,4096,128]{2,1,0:T(8,128)S(1)} fusion(f32[512,4096]{1,0:T(8,128)S(1)} %get-tuple-element.145, f32[4096]{0:T(1024)S(1)} %bitcast.97, pred[512]{0:T(512)(128)(4,1)S(1)} %add_compare_fusion.3, f32[1,4096,128]{2,1,0:T(8,128)S(1)} %get-tuple-element.164, f32[4096]{0:T(1024)S(1)} %bitcast.111, ...), kind=kOutput, calls=%fused_computation.6.clone.1 | convolution fusion | flops 546308096 | bytes 12747268 | tf_op jit(solution)/shard_map/while/body/grk,gkd->grd/dot_general | solution.py:22
  85.8 2.3 fusion.41
  88.1 2.1 fusion.42
  90.2 4.3 %fusion.43 = f32[1,4096,128]{2,1,0:T(8,128)S(1)} fusion(f32[512,4096]{1,0:T(8,128)S(1)} %get-tuple-element.145, f32[4096]{0:T(1024)S(1)} %bitcast.97, pred[512]{0:T(512)(128)(4,1)S(1)} %add_compare_fusion.3, f32[1,4096,128]{2,1,0:T(8,128)S(1)} %get-tuple-element.164, f32[4096]{0:T(1024)S(1)} %bitcast.111, ...), kind=kOutput, calls=%fused_computation.6.clone.1 | convolution fusion | flops 546308096 | bytes 12747268 | tf_op jit(solution)/shard_map/while/body/grk,gkd->grd/dot_general | solution.py:22
  94.6 2.3 fusion.41
  96.9 2.1 fusion.42
  99.0 4.3 %fusion.43 = f32[1,4096,128]{2,1,0:T(8,128)S(1)} fusion(f32[512,4096]{1,0:T(8,128)S(1)} %get-tuple-element.145, f32[4096]{0:T(1024)S(1)} %bitcast.97, pred[512]{0:T(512)(128)(4,1)S(1)} %add_compare_fusion.3, f32[1,4096,128]{2,1,0:T(8,128)S(1)} %get-tuple-element.164, f32[4096]{0:T(1024)S(1)} %bitcast.111, ...), kind=kOutput, calls=%fused_computation.6.clone.1 | convolution fusion | flops 546308096 | bytes 12747268 | tf_op jit(solution)/shard_map/while/body/grk,gkd->grd/dot_general | solution.py:22
  103.4 2.3 fusion.41
  105.7 2.1 fusion.42
  107.8 4.3 %fusion.43 = f32[1,4096,128]{2,1,0:T(8,128)S(1)} fusion(f32[512,4096]{1,0:T(8,128)S(1)} %get-tuple-element.145, f32[4096]{0:T(1024)S(1)} %bitcast.97, pred[512]{0:T(512)(128)(4,1)S(1)} %add_compare_fusion.3, f32[1,4096,128]{2,1,0:T(8,128)S(1)} %get-tuple-element.164, f32[4096]{0:T(1024)S(1)} %bitcast.111, ...), kind=kOutput, calls=%fused_computation.6.clone.1 | convolution fusion | flops 546308096 | bytes 12747268 | tf_op jit(solution)/shard_map/while/body/grk,gkd->grd/dot_general | solution.py:22
  112.2 2.3 fusion.41
  114.5 2.1 fusion.42
  116.6 4.3 %fusion.43 = f32[1,4096,128]{2,1,0:T(8,128)S(1)} fusion(f32[512,4096]{1,0:T(8,128)S(1)} %get-tuple-element.145, f32[4096]{0:T(1024)S(1)} %bitcast.97, pred[512]{0:T(512)(128)(4,1)S(1)} %add_compare_fusion.3, f32[1,4096,128]{2,1,0:T(8,128)S(1)} %get-tuple-element.164, f32[4096]{0:T(1024)S(1)} %bitcast.111, ...), kind=kOutput, calls=%fused_computation.6.clone.1 | convolution fusion | flops 546308096 | bytes 12747268 | tf_op jit(solution)/shard_map/while/body/grk,gkd->grd/dot_general | solution.py:22
  121.0 2.3 fusion.41
  123.3 2.1 fusion.42
  125.5 4.3 %fusion.43 = f32[1,4096,128]{2,1,0:T(8,128)S(1)} fusion(f32[512,4096]{1,0:T(8,128)S(1)} %get-tuple-element.145, f32[4096]{0:T(1024)S(1)} %bitcast.97, pred[512]{0:T(512)(128)(4,1)S(1)} %add_compare_fusion.3, f32[1,4096,128]{2,1,0:T(8,128)S(1)} %get-tuple-element.164, f32[4096]{0:T(1024)S(1)} %bitcast.111, ...), kind=kOutput, calls=%fused_computation.6.clone.1 | convolution fusion | flops 546308096 | bytes 12747268 | tf_op jit(solution)/shard_map/while/body/grk,gkd->grd/dot_general | solution.py:22
  129.8 2.3 fusion.41
  132.1 2.1 fusion.42
  134.3 4.3 %fusion.43 = f32[1,4096,128]{2,1,0:T(8,128)S(1)} fusion(f32[512,4096]{1,0:T(8,128)S(1)} %get-tuple-element.145, f32[4096]{0:T(1024)S(1)} %bitcast.97, pred[512]{0:T(512)(128)(4,1)S(1)} %add_compare_fusion.3, f32[1,4096,128]{2,1,0:T(8,128)S(1)} %get-tuple-element.164, f32[4096]{0:T(1024)S(1)} %bitcast.111, ...), kind=kOutput, calls=%fused_computation.6.clone.1 | convolution fusion | flops 546308096 | bytes 12747268 | tf_op jit(solution)/shard_map/while/body/grk,gkd->grd/dot_general | solution.py:22
  138.6 2.3 fusion.41
  140.9 2.1 fusion.42
  143.1 4.3 %fusion.43 = f32[1,4096,128]{2,1,0:T(8,128)S(1)} fusion(f32[512,4096]{1,0:T(8,128)S(1)} %get-tuple-element.145, f32[4096]{0:T(1024)S(1)} %bitcast.97, pred[512]{0:T(512)(128)(4,1)S(1)} %add_compare_fusion.3, f32[1,4096,128]{2,1,0:T(8,128)S(1)} %get-tuple-element.164, f32[4096]{0:T(1024)S(1)} %bitcast.111, ...), kind=kOutput, calls=%fused_computation.6.clone.1 | convolution fusion | flops 546308096 | bytes 12747268 | tf_op jit(solution)/shard_map/while/body/grk,gkd->grd/dot_general | solution.py:22
  147.4 2.3 fusion.41
  149.7 2.1 fusion.42
  151.9 4.3 %fusion.43 = f32[1,4096,128]{2,1,0:T(8,128)S(1)} fusion(f32[512,4096]{1,0:T(8,128)S(1)} %get-tuple-element.145, f32[4096]{0:T(1024)S(1)} %bitcast.97, pred[512]{0:T(512)(128)(4,1)S(1)} %add_compare_fusion.3, f32[1,4096,128]{2,1,0:T(8,128)S(1)} %get-tuple-element.164, f32[4096]{0:T(1024)S(1)} %bitcast.111, ...), kind=kOutput, calls=%fused_computation.6.clone.1 | convolution fusion | flops 546308096 | bytes 12747268 | tf_op jit(solution)/shard_map/while/body/grk,gkd->grd/dot_general | solution.py:22
  156.5 4.5 %fusion.18 = f32[4096]{0:T(1024)S(1)} fusion(f32[4096,512]{0,1:T(8,128)} %get-tuple-element.83, f32[4096]{0:T(1024)S(1)} %bitcast.113), kind=kLoop, calls=%fused_computation.27 | loop fusion | flops 4190208 | bytes 8421376 | tf_op jit(solution)/shard_map/reduce_sum | solution.py:21
  161.1 4.7 %fusion.22 = bf16[1,4096,128]{2,1,0:T(8,128)(2,1)S(1)} fusion(bf16[512,128]{1,0:T(8,128)(2,1)S(1)} %bitcast.115, f32[4096,512]{0,1:T(8,128)} %get-tuple-element.83, f32[4096]{0:T(1024)S(1)} %bitcast.114, f32[1,4096,128]{2,1,0:T(8,128)S(1)} %get-tuple-element.55, f32[4096]{0:T(1024)S(1)} %bitcast.119, f32[4096]{0:T(1024)S(1)} %bitcast.120), kind=kOutput, calls=%fused_computation.32 | convolution fusion | flops 543162368 | bytes 11714560 | tf_op jit(solution)/shard_map/grk,gkd->grd/dot_general | solution.py:22
  165.8 0.5 copy.36
  166.3 17.0 %convolution_convert_fusion = bf16[512,8192]{1,0:T(8,128)(2,1)} fusion(bf16[512,1024]{0,1:T(8,128)(2,1)S(1)} %bitcast.108, bf16[1024,8192]{1,0:T(8,128)(2,1)} %all-gather.2.cloned.1.call-done), kind=kOutput, calls=%fused_computation.23 | convolution fusion | flops 8594128896 | bytes 26214400 | tf_op jit(solution)/shard_map/dot_general | solution.py:103
  183.3 0.6 copy-done.1
  183.9 0.6 dynamic_slice.13
  184.5 0.7 add_compare_fusion.1
  185.2 136.6 %reduce-scatter.2.cloned.1.call-done = bf16[128,8192]{1,0:T(8,128)(2,1)} async-done(((bf16[512,8192]{1,0:T(8,128)(2,1)}), bf16[128,8192]{1,0:T(8,128)(2,1)}) %reduce-scatter.2.cloned.1.call-update) | async-done | bytes 2097168 | tf_op jit(solution)/shard_map/reduce_scatter | solution.py:108
  321.8 3.1 select_bitcast_fusion
  (52 shorter events, 1.2 us)
Async XLA Ops:
  6.5 50.9 %copy-start = (s32[32]{0:T(128)S(1)}, s32[32]{0:T(128)}, u32[]{:S(2)}) copy-start(s32[32]{0:T(128)} %param.16) | copy-start | bytes 388
  6.5 159.8 %all-gather.2.cloned.1.call-start = ((), (), s32[]{:S(2)}) async-start(), calls=%async_computation.4 | async-start | bytes 17301504 | tf_op jit(solution)/shard_map/all_gather | solution.py:105
  11.1 9.7 %all-to-all-start.1 = ((bf16[4,2,8192]{2,1,0:T(2,128)(2,1)}), bf16[4,2,8192]{2,1,0:T(2,128)(2,1)S(1)}, u32[]{:S(2)}, u32[]{:S(2)}) async-start(bf16[4,2,8192]{2,1,0:T(2,128)(2,1)} %reshape.99), calls=%async_computation.1 | async-start | bytes 262144 | tf_op jit(solution)/shard_map/all_to_all | solution.py:71
  20.7 32.5 %all-to-all-start.2 = ((bf16[4,2,8192]{2,1,0:T(2,128)(2,1)}), bf16[4,2,8192]{2,1,0:T(2,128)(2,1)S(1)}, u32[]{:S(2)}, u32[]{:S(2)}) async-start(bf16[4,2,8192]{2,1,0:T(2,128)(2,1)} %reshape.95), calls=%async_computation.2 | async-start | bytes 262144 | tf_op jit(solution)/shard_map/all_to_all | solution.py:72
  53.2 16.5 %all-to-all-start = ((bf16[4,2,65536]{2,1,0:T(2,128)(2,1)}), bf16[4,2,65536]{2,1,0:T(2,128)(2,1)S(1)}, u32[]{:S(2)}, u32[]{:S(2)}) async-start(bf16[4,2,65536]{2,1,0:T(2,128)(2,1)} %reshape.97), calls=%async_computation | async-start | bytes 2097152 | tf_op jit(solution)/shard_map/all_to_all | solution.py:70
  57.4 264.4 %reduce-scatter.2.cloned.1.call-start = ((), (), s32[]{:S(2)}) async-start(), calls=%async_computation.5 | async-start | bytes 10485760 | tf_op jit(solution)/shard_map/reduce_scatter | solution.py:108
  183.3 0.7 copy-start.1
Sparse Core Ops, SparseCore 0:
  9.5 83.7 all-gather.1
  183.4 138.3 reduce-scatter.1
where the time goes:
time: 336 us; the launch traced here: 332 us
  waiting for transfers between devices  150 us (45%)
  matrix products  85.5 us (25%)
  other arithmetic  53.3 us (16%)
  local copies, waits for them, and re-layouts  15.9 us (5%)
  between operations  14.2 us (4%)
  starting transfers between devices  12.4 us (4%)
    reduce_scatter x1, waiting for transfers between devices, local(): lax.psum_scatter(terms.astype(jnp.bfloat16), 'sp', scatter_dimension=0, t...  137 us
    dot_general x10, matrix products, block_update(): jnp.einsum('grk,gkd->grd', weights.astype(jnp.bfloat16), value_block, pre...  43.4 us
    unnamed x3, other arithmetic  25.3 us
    dot_general x10, matrix products, block_update(): jnp.einsum('grd,gkd->grk', query_rows, key_block, preferred_element_type=...  25.1 us
    reduce_sum x10, other arithmetic, block_update(): running_sum = running_sum * rescale + jnp.sum(weights, axis=-1)  23.3 us
    dot_general x1, matrix products, local(): jnp.dot(attended, lax.all_gather(out_weight, 'dp', axis=1, tiled=True), p...  17 us
    unnamed x18, local copies, waits for them, and re-layouts  13.1 us
    all_to_all x1, waiting for transfers between devices, local(): lax.all_to_all(queries, 'sp', split_axis=2, concat_axis=1, tiled=True)  10.5 us
  transfers between devices with their start and end apart: 5, of which 3 were waited for; matrix products, arithmetic and copies ran while one was open for 40% of the time, Pallas kernels for 0%

commit v1 on v0

v1 whole, which is shorter than its diff:
```python
import functools
import math

import jax
import jax.numpy as jnp
from jax import lax
from jax.experimental import pallas as pl
from jax.experimental.pallas import tpu as pltpu
from jax.sharding import PartitionSpec as P

NEGATIVE = -1e30
VMEM_LIMIT = 48 << 20
KEY_BLOCK = 4096
ROW_CHUNK = 128


def attention_kernel(
    scalars, q_ref, s0_ref, s1_ref, s2_ref, s3_ref, k_ref, v_ref, o_ref, rows, span, high, total, *, factor
):
    step = pl.program_id(0)
    head_dim = k_ref.shape[1]
    positions = q_ref.shape[0]
    heads = q_ref.shape[1] // head_dim
    row_count = heads * positions
    key_block = k_ref.shape[0]
    chunk = min(ROW_CHUNK, row_count)
    length = scalars[0]
    first_position = scalars[2]
    live = first_position < scalars[1]

    def update(keys, values, usable):
        augmented = jnp.concatenate([values, jnp.ones_like(values)], axis=1)

        def score(start):
            return lax.dot_general(
                rows[start : start + chunk, :],
                keys,
                (((1,), (1,)), ((), ())),
                preferred_element_type=jnp.float32,
            )

        following = score(0)
        for start in range(0, row_count, chunk):
            scores = following
            if start + chunk < row_count:
                following = score(start + chunk)
            if usable is not None:
                scores = jnp.where(usable(start, scores.shape), scores, NEGATIVE)
            block = pl.ds(start, chunk)
            before = high[block, :]
            after = jnp.maximum(before, jnp.max(scores, axis=1, keepdims=True))
            high[block, :] = after
            rescale = jnp.exp2((before - after) * factor)
            weights = jnp.exp2((scores - after[:, :1]) * factor).astype(jnp.bfloat16)
            total[block, :] = total[block, :] * jnp.concatenate([rescale, rescale], axis=1) + jnp.dot(
                weights, augmented, preferred_element_type=jnp.float32
            )

    @pl.when(jnp.logical_and(step == 0, live))
    def _():
        for head in range(heads):
            rows[head * positions : (head + 1) * positions, :] = q_ref[:, head * head_dim : (head + 1) * head_dim]
        high[...] = jnp.full_like(high, NEGATIVE)
        total[...] = jnp.zeros_like(total)
        width = s0_ref.shape[0]
        for index, source in enumerate((s0_ref, s1_ref, s2_ref, s3_ref)):
            span[index * width : (index + 1) * width, :] = source[...]

        def causal(start, shape):
            query = first_position + (start + lax.broadcasted_iota(jnp.int32, shape, 0)) % positions
            column = lax.broadcasted_iota(jnp.int32, shape, 1)
            key = scalars[3] + column
            for index in range(1, 4):
                key = jnp.where(column >= index * width, scalars[3 + index] + column - index * width, key)
            return key <= query

        update(span[:, :head_dim], span[:, head_dim:], causal)

    before_block = (step - 1) * key_block

    @pl.when(jnp.logical_and(live, jnp.logical_and(step > 0, step * key_block <= length)))
    def _():
        update(k_ref[...], v_ref[...], None)

    @pl.when(
        jnp.logical_and(
            live,
            jnp.logical_and(step > 0, jnp.logical_and(before_block < length, step * key_block > length)),
        )
    )
    def _():
        def stored(start, shape):
            return before_block + lax.broadcasted_iota(jnp.int32, shape, 1) < length

        update(k_ref[...], v_ref[...], stored)

    @pl.when(step == pl.num_programs(0) - 1)
    def _():
        @pl.when(live)
        def _():
            for head in range(heads):
                block = slice(head * positions, (head + 1) * positions)
                o_ref[:, head * head_dim : (head + 1) * head_dim] = (
                    total[block, :head_dim] / total[block, head_dim:]
                ).astype(o_ref.dtype)

        @pl.when(jnp.logical_not(live))
        def _():
            o_ref[...] = jnp.zeros_like(o_ref)


def attend(scalars, query, fresh, keys, values):
    positions, features = query.shape
    stored, head_dim = keys.shape
    key_block = math.gcd(KEY_BLOCK, stored)
    blocks = stored // key_block
    row_count = positions * features // head_dim
    width = fresh[0].shape[0]

    def cached(step, scalars):
        last = lax.div(scalars[0] - 1, key_block)
        return (jnp.clip(step - 1, 0, last), 0)

    def whole(step, scalars):
        return (0, 0)

    flops = 4 * row_count * (stored + 4 * width) * head_dim * 2
    return pl.pallas_call(
        functools.partial(attention_kernel, factor=math.log2(math.e) / math.sqrt(head_dim)),
        grid_spec=pltpu.PrefetchScalarGridSpec(
            num_scalar_prefetch=1,
            grid=(blocks + 1,),
            in_specs=[pl.BlockSpec((positions, features), whole)]
            + [pl.BlockSpec((width, 2 * head_dim), whole)] * 4
            + [pl.BlockSpec((key_block, head_dim), cached)] * 2,
            out_specs=pl.BlockSpec((positions, features), whole),
            scratch_shapes=[
                pltpu.VMEM((row_count, head_dim), jnp.bfloat16),
                pltpu.VMEM((4 * width, 2 * head_dim), jnp.bfloat16),
                pltpu.VMEM((row_count, head_dim), jnp.float32),
                pltpu.VMEM((row_count, 2 * head_dim), jnp.float32),
            ],
        ),
        out_shape=jax.ShapeDtypeStruct((positions, features), jnp.bfloat16),
        compiler_params=pltpu.CompilerParams(vmem_limit_bytes=VMEM_LIMIT),
        cost_estimate=pl.CostEstimate(
            flops=flops, bytes_accessed=4 * stored * head_dim, transcendentals=row_count * stored
        ),
        name="attend",
    )(scalars, query, *fresh, keys, values)


def project_kernel(*refs, column_blocks, added, outs):
    mine_ref, other_ref, w_ref = refs[:3]
    add_refs = refs[3 : 3 + len(added)]
    out_refs = refs[3 + len(added) : 3 + len(added) + outs]
    step = pl.program_id(0)
    width = w_ref.shape[2]
    positions = mine_ref.shape[0]
    for index in range(column_blocks):
        columns = slice(index * width, (index + 1) * width)
        for half, source in enumerate((mine_ref, other_ref)):
            block = slice(half * positions, (half + 1) * positions)
            product = jnp.dot(source[...], w_ref[index], preferred_element_type=jnp.float32)
            for (low, high), add_ref in zip(added, add_refs):
                inside = jnp.logical_and(step >= low, step < high)
                product = product + jnp.where(inside, add_ref[block, columns].astype(jnp.float32), 0.0)
            if outs == 1:
                out_refs[0][block, columns] = product.astype(jnp.bfloat16)
            else:
                steps = pl.num_programs(0)
                for part in range(outs):

                    @pl.when(step * outs // steps == part)
                    def _(product=product, part=part):
                        out_refs[part][block, columns] = product.astype(jnp.bfloat16)


def project(mine, other, weight, added=(), outs=1):
    positions, depth = mine.shape
    blocks, _, width = weight.shape
    column_blocks = 2
    steps = blocks // column_blocks
    tile = column_blocks * width
    rows = 2 * positions

    def within(low, high):
        return lambda step: (0, jnp.clip(step - low, 0, high - low - 1))

    share = steps // outs
    out = pl.pallas_call(
        functools.partial(
            project_kernel, column_blocks=column_blocks, added=[(low, high) for _, low, high in added], outs=outs
        ),
        grid=(steps,),
        in_specs=[
            pl.BlockSpec((positions, depth), lambda step: (0, 0)),
            pl.BlockSpec((positions, depth), lambda step: (0, 0)),
            pl.BlockSpec((column_blocks, depth, width), lambda step: (step, 0, 0)),
        ]
        + [pl.BlockSpec((rows, tile), within(low, high)) for _, low, high in added],
        out_specs=[pl.BlockSpec((rows, tile), within(part * share, (part + 1) * share)) for part in range(outs)],
        out_shape=[jax.ShapeDtypeStruct((rows, share * tile), jnp.bfloat16) for _ in range(outs)],
        compiler_params=pltpu.CompilerParams(vmem_limit_bytes=VMEM_LIMIT),
        cost_estimate=pl.CostEstimate(
            flops=2 * rows * depth * blocks * width, bytes_accessed=2 * depth * blocks * width, transcendentals=0
        ),
        name="project",
    )(mine, other, weight, *[array for array, _, _ in added])
    return out


def combine_kernel(scalars, even_ref, odd_ref, o_ref, *, width):
    positions = even_ref.shape[0]
    keep = scalars[1] + lax.broadcasted_iota(jnp.int32, (positions, width), 0) < scalars[0]
    zero = jnp.zeros((positions, width), jnp.bfloat16)
    own, arrived = even_ref, odd_ref
    flip = scalars[2] == 1
    for index in range(own.shape[1] // width):
        columns = slice(index * width, (index + 1) * width)
        first = jnp.where(keep, own[:, columns], zero)
        second = jnp.where(keep, arrived[:, columns], zero)
        left = jnp.where(flip, second, first)
        right = jnp.where(flip, first, second)
        o_ref[0, :, 2 * index * width : (2 * index + 1) * width] = left
        o_ref[0, :, (2 * index + 1) * width : (2 * index + 2) * width] = right


def combine(scalars, own, arrived, width):
    positions, columns = own.shape
    steps = 4
    tile = columns // steps
    return pl.pallas_call(
        functools.partial(combine_kernel, width=width),
        grid_spec=pltpu.PrefetchScalarGridSpec(
            num_scalar_prefetch=1,
            grid=(steps,),
            in_specs=[pl.BlockSpec((positions, tile), lambda step, scalars: (0, step))] * 2,
            out_specs=pl.BlockSpec((1, positions, 2 * tile), lambda step, scalars: (0, 0, step)),
        ),
        out_shape=jax.ShapeDtypeStruct((1, positions, 2 * columns), jnp.bfloat16),
        compiler_params=pltpu.CompilerParams(vmem_limit_bytes=VMEM_LIMIT),
        name="combine",
    )(scalars, own, arrived)


def local(
    queries,
    rotated_span_keys,
    span_value_heads,
    cache_keys,
    cached_prefix_values,
    out_weight,
    prefix_lengths,
    valid_lengths,
):
    parts = lax.axis_size("sp")
    rows = lax.axis_size("dp")
    me = lax.axis_index("sp")
    row = lax.axis_index("dp")
    positions = queries.shape[1]
    head_dim = cache_keys.shape[3]
    features = queries.shape[2] // parts

    same_core = [list(range(core, rows, 2)) for core in range(2)]
    weight = lax.all_gather(out_weight, "dp", axis=0, tiled=False, axis_index_groups=same_core)

    def shift(array, distance):
        return lax.ppermute(array, "sp", [(i, (i + distance) % parts) for i in range(parts)])

    def swap(array):
        return lax.ppermute(array, "dp", [(i, i ^ 1) for i in range(rows)])

    def part_of(array, owner, size):
        return lax.dynamic_slice_in_dim(array, owner * size, size, 1)

    position = [(me + distance) % parts for distance in range(parts)]
    fresh_parts, query_parts = [], []
    for distance in range(parts):
        owner = position[distance]
        pair = jnp.concatenate(
            [
                part_of(rotated_span_keys[0], owner, head_dim),
                part_of(span_value_heads[0], owner, head_dim),
            ],
            axis=1,
        )
        fresh_parts.append(pair if distance == 0 else shift(pair, distance))
    for distance in range(parts):
        part = part_of(queries[0], position[distance], features)
        query_parts.append(part if distance == 0 else shift(part, distance))
    fresh = [fresh_parts[(parts - distance) % parts] for distance in range(parts)]
    query = [query_parts[(parts - distance) % parts] for distance in range(parts)]

    own_prefix = lax.dynamic_index_in_dim(prefix_lengths, row, 0, keepdims=False)
    own_valid = lax.dynamic_index_in_dim(valid_lengths, row, 0, keepdims=False)
    starts = [place * positions for place in position]

    def attended(distance, begin, size):
        scalars = jnp.stack([own_prefix, own_valid, starts[distance] + begin] + starts).astype(jnp.int32)
        block = lax.slice_in_dim(query[distance], begin, begin + size, axis=0)
        mine = attend(scalars, block, fresh, cache_keys[0, 0], cached_prefix_values[0, 0])
        return mine, swap(mine)

    half = positions // 2
    steps = weight.shape[0] // 2

    far = attended(2, 0, positions)
    send_right, send_left = project(*far, weight, outs=2)
    from_left, from_right = shift(send_right, 1), shift(send_left, -1)

    def rows_of(array, begin):
        return jnp.concatenate(
            [array[begin : begin + half], array[positions + begin : positions + begin + half]], axis=0
        )

    arrived = []
    for begin in (0, half):
        right = attended(1, begin, half)
        (to_right,) = project(*right, weight, added=[(rows_of(from_left, begin), 0, steps // 2)])
        right_in = shift(to_right, 1)
        left = attended(3, begin, half)
        (to_left,) = project(*left, weight, added=[(rows_of(from_right, begin), steps // 2, steps)])
        left_in = shift(to_left, -1)
        arrived.append((right_in, left_in))

    results = []
    own = attended(0, 0, positions)
    (total,) = project(*own, weight)
    scalars = jnp.stack([own_valid, starts[0], row % 2]).astype(jnp.int32)
    for index, begin in enumerate((0, half)):
        first, second = arrived[index]
        summed = (
            rows_of(total, begin).astype(jnp.float32) + first.astype(jnp.float32) + second.astype(jnp.float32)
        ).astype(jnp.bfloat16)
        results.append(summed)
    mine = jnp.concatenate([results[0][:half], results[1][:half]], axis=0)
    theirs = jnp.concatenate([results[0][half:], results[1][half:]], axis=0)
    return combine(scalars, mine, swap(theirs), weight.shape[2])


def solution(mesh):
    in_specs = (
        P("dp", "sp", None),
        P("dp", "sp", None),
        P("dp", "sp", None),
        P("dp", "sp", None, None),
        P("dp", "sp", None, None),
        P("sp", "dp"),
        P(),
        P(),
    )
    out_specs = P("dp", "sp", None)
    return jax.shard_map(local, mesh=mesh, in_specs=in_specs, out_specs=out_specs, check_vma=False)
```

time: 336 us -> 203 us (0.60)
  the two profiles are of different devices: /device:TPU:1 before, /device:TPU:23 now
where the time goes in v1:
time: 203 us; the launch traced here: 200 us
  Pallas kernels  93.9 us (46%)
  waiting for transfers between devices  39.7 us (20%)
  starting transfers between devices  35.5 us (17%)
  local copies, waits for them, and re-layouts  14.6 us (7%)
  between operations  14.1 us (7%)
  other arithmetic  2.09 us (1%)
    pallas_call x6, Pallas kernels, project(): pl.pallas_call(functools.partial(project_kernel, column_blocks=column_blo...  49.7 us
    pallas_call x6, Pallas kernels, attend(): pl.pallas_call(functools.partial(attention_kernel, factor=math.log2(math....  41.7 us
    ppermute x12, waiting for transfers between devices, shift(): lax.ppermute(array, 'sp', [(i, (i + distance) % parts) for i in range(par...  28.4 us
    ppermute x7, starting transfers between devices, swap(): return lax.ppermute(array, 'dp', [(i, i ^ 1) for i in range(rows)])  22.6 us
    ppermute x12, starting transfers between devices, shift(): lax.ppermute(array, 'sp', [(i, (i + distance) % parts) for i in range(par...  12.9 us
    all_gather x1, waiting for transfers between devices, local(): lax.all_gather(out_weight, 'dp', axis=0, tiled=False, axis_index_groups=s...  9.15 us
    another operation x6, local copies, waits for them, and re-layouts, attended(): jnp.stack([own_prefix, own_valid, starts[distance] + begin] + starts)  8.5 us
  transfers between devices with their start and end apart: 20, of which 5 were waited for; matrix products, arithmetic and copies ran while one was open for 6% of the time, Pallas kernels for 46%

profile of v1, /device:TPU:23, one launch (start us, length us, event | category | flops | bytes accessed | tf_op | source)
XLA Modules:
  0.0 199.8 jit_solution(10750859657682931323)
XLA Ops:
  6.5 0.7 all-gather.3.cloned.1.call-update
  7.3 0.9 dynamic-slice_bitcast_fusion.4
  8.3 1.2 collective-permute-start.1
  9.5 0.1 collective-permute-start
  9.6 2.7 %collective-permute-start.2 = (bf16[128,256]{1,0:T(8,128)(2,1)S(1)}, bf16[128,256]{1,0:T(8,128)(2,1)S(1)}, u32[]{:S(2)}, u32[]{:S(2)}) collective-permute-start(bf16[128,256]{1,0:T(8,128)(2,1)S(1)} %pad_maximum_fusion.9), channel_id=1, source_target_pairs={{0,1},{1,2},{2,3},{3,0},{4,5},{5,6},{6,7},{7,4},{8,9},{9,10},{10,1... | collective-permute-start | bytes 196616 | tf_op jit(solution)/shard_map/ppermute | solution.py:269
  12.3 0.1 dynamic-slice_bitcast_fusion.3
  12.4 0.1 collective-permute-start.4
  12.5 2.7 %collective-permute-start.10 = (bf16[128,1024]{1,0:T(8,128)(2,1)S(1)}, bf16[128,1024]{1,0:T(8,128)(2,1)S(1)}, u32[]{:S(2)}, u32[]{:S(2)}) collective-permute-start(bf16[128,1024]{1,0:T(8,128)(2,1)S(1)} %get-tuple-element.27), channel_id=1, source_target_pairs={{0,1},{1,2},{2,3},{3,0},{4,5},{5,6},{6,7},{7,4},{8,9},{9,10},{10,1... | collective-permute-start | bytes 786440 | tf_op jit(solution)/shard_map/ppermute | solution.py:269
  15.1 0.7 dynamic_slice.67
  15.8 0.6 dynamic_slice.68
  16.4 1.4 stack.37.scalars
  17.8 1.4 stack.36.scalars
  19.2 1.4 stack.35.scalars
  20.6 1.4 stack.34.scalars
  22.0 1.4 stack.41.scalars
  23.5 1.4 stack.39.scalars
  24.9 0.0 collective-permute-done.1.s2_ref
  24.9 0.1 collective-permute-start.6
  25.0 0.0 collective-permute-done.s1_ref
  25.0 0.0 collective-permute-done.2.s3_ref
  25.0 0.0 copy-start
  25.0 1.6 copy-done
  26.6 1.6 copy-done.2
  28.3 13.9 %attend.6.refs_0_ = bf16[128,1024]{1,0:T(8,128)(2,1)S(1)} custom-call(s32[7]{0:T(128)S(1)} %stack.34.scalars, bf16[128,1024]{1,0:T(8,128)(2,1)S(1)} %get-tuple-element.25.q_ref, bf16[128,256]{1,0:T(8,128)(2,1)S(1)} %pad_maximum_fusion.6.s0_ref, bf16[128,256]{1,0:T(8,128)(2,1)S(1)} %collective-permute-done.s1_ref, ...), custom_call_target="tpu_custom_call" | custom-call | flops 9126805504 | bytes 4194304 | tf_op jit(solution)/shard_map/attend/pallas_call | solution.py:128
  42.2 2.1 %collective-permute-start.3 = (bf16[128,1024]{1,0:T(8,128)(2,1)S(1)}, bf16[128,1024]{1,0:T(8,128)(2,1)S(1)}, u32[]{:S(2)}, u32[]{:S(2)}) collective-permute-start(bf16[128,1024]{1,0:T(8,128)(2,1)S(1)} %attend.6.refs_0_), channel_id=1, source_target_pairs={{0,4},{4,0},{8,12},{12,8},{16,20},{20,16},{24,28},{28,24},{32,36},... | collective-permute-start | bytes 786440 | tf_op jit(solution)/shard_map/ppermute | solution.py:272
  44.3 4.7 %attend.10.refs_0_ = bf16[64,1024]{1,0:T(8,128)(2,1)S(1)} custom-call(s32[7]{0:T(128)S(1)} %stack.39.scalars, bf16[64,1024]{1,0:T(8,128)(2,1)S(1)} %get-tuple-element.30.q_ref, bf16[128,256]{1,0:T(8,128)(2,1)S(1)} %pad_maximum_fusion.6.s0_ref, bf16[128,256]{1,0:T(8,128)(2,1)S(1)} %collective-permute-done.s1_ref, ...), custom_call_target="tpu_custom_call" | custom-call | flops 4563402752 | bytes 4194304 | tf_op jit(solution)/shard_map/attend/pallas_call | solution.py:128
  49.0 3.0 %collective-permute-start.14 = (bf16[64,1024]{1,0:T(8,128)(2,1)S(1)}, bf16[64,1024]{1,0:T(8,128)(2,1)S(1)}, u32[]{:S(2)}, u32[]{:S(2)}) collective-permute-start(bf16[64,1024]{1,0:T(8,128)(2,1)S(1)} %attend.10.refs_0_), channel_id=1, source_target_pairs={{0,4},{4,0},{8,12},{12,8},{16,20},{20,16},{24,28},{28,24},{32,36},... | collective-permute-start | bytes 393224 | tf_op jit(solution)/shard_map/ppermute | solution.py:272
  52.0 8.3 %attend.8.refs_0_ = bf16[128,1024]{1,0:T(8,128)(2,1)S(1)} custom-call(s32[7]{0:T(128)S(1)} %stack.36.scalars, bf16[128,1024]{1,0:T(8,128)(2,1)S(1)} %collective-permute-done.6.q_ref, bf16[128,256]{1,0:T(8,128)(2,1)S(1)} %pad_maximum_fusion.6.s0_ref, bf16[128,256]{1,0:T(8,128)(2,1)S(1)} %collective-permute-done.s1_ref, ...), custom_call_target="tpu_custom_call" | custom-call | flops 9126805504 | bytes 4194304 | tf_op jit(solution)/shard_map/attend/pallas_call | solution.py:128
  60.3 5.2 %collective-permute-start.7 = (bf16[128,1024]{1,0:T(8,128)(2,1)S(1)}, bf16[128,1024]{1,0:T(8,128)(2,1)S(1)}, u32[]{:S(2)}, u32[]{:S(2)}) collective-permute-start(bf16[128,1024]{1,0:T(8,128)(2,1)S(1)} %attend.8.refs_0_), channel_id=1, source_target_pairs={{0,4},{4,0},{8,12},{12,8},{16,20},{20,16},{24,28},{28,24},{32,36},... | collective-permute-start | bytes 786440 | tf_op jit(solution)/shard_map/ppermute | solution.py:272
  65.6 4.7 %attend.7.refs_0_ = bf16[64,1024]{1,0:T(8,128)(2,1)S(1)} custom-call(s32[7]{0:T(128)S(1)} %stack.35.scalars, bf16[64,1024]{1,0:T(8,128)(2,1)S(1)} %get-tuple-element.29.q_ref, bf16[128,256]{1,0:T(8,128)(2,1)S(1)} %pad_maximum_fusion.6.s0_ref, bf16[128,256]{1,0:T(8,128)(2,1)S(1)} %collective-permute-done.s1_ref, ...), custom_call_target="tpu_custom_call" | custom-call | flops 4563402752 | bytes 4194304 | tf_op jit(solution)/shard_map/attend/pallas_call | solution.py:128
  70.3 2.9 %collective-permute-start.5 = (bf16[64,1024]{1,0:T(8,128)(2,1)S(1)}, bf16[64,1024]{1,0:T(8,128)(2,1)S(1)}, u32[]{:S(2)}, u32[]{:S(2)}) collective-permute-start(bf16[64,1024]{1,0:T(8,128)(2,1)S(1)} %attend.7.refs_0_), channel_id=1, source_target_pairs={{0,4},{4,0},{8,12},{12,8},{16,20},{20,16},{24,28},{28,24},{32,36},... | collective-permute-start | bytes 393224 | tf_op jit(solution)/shard_map/ppermute | solution.py:272
  73.3 9.2 %all-gather.3.cloned.1.call-done = bf16[16384,256]{1,0:T(8,128)(2,1)} async-done(((bf16[1024,256]{1,0:T(8,128)(2,1)}), bf16[16384,256]{1,0:T(8,128)(2,1)}) %all-gather.3.cloned.1.call-update) | async-done | bytes 8388624 | tf_op jit(solution)/shard_map/all_gather | solution.py:266
  82.4 11.1 %project.7 = (bf16[256,2048]{1,0:T(8,128)(2,1)S(1)}, bf16[256,2048]{1,0:T(8,128)(2,1)S(1)}) custom-call(bf16[128,1024]{1,0:T(8,128)(2,1)S(1)} %attend.8.refs_0_, bf16[128,1024]{1,0:T(8,128)(2,1)S(1)} %collective-permute-done.7.refs_1_, bf16[16,1024,256]{2,1,0:T(8,128)(2,1)} %bitcast.46), custom_call_target="tpu_custom_call" | custom-call | flops 2147483648 | bytes 8388608 | tf_op jit(solution)/shard_map/project/pallas_call | solution.py:191
  93.5 0.3 collective-permute-start.8
  93.8 4.9 %attend.9.refs_0_ = bf16[64,1024]{1,0:T(8,128)(2,1)S(1)} custom-call(s32[7]{0:T(128)S(1)} %stack.37.scalars, bf16[64,1024]{1,0:T(8,128)(2,1)S(1)} %get-tuple-element.31.q_ref, bf16[128,256]{1,0:T(8,128)(2,1)S(1)} %pad_maximum_fusion.6.s0_ref, bf16[128,256]{1,0:T(8,128)(2,1)S(1)} %collective-permute-done.s1_ref, ...), custom_call_target="tpu_custom_call" | custom-call | flops 4563402752 | bytes 4194304 | tf_op jit(solution)/shard_map/attend/pallas_call | solution.py:128
  98.7 1.3 collective-permute-start.12
  100.0 5.1 %attend.11.refs_0_ = bf16[64,1024]{1,0:T(8,128)(2,1)S(1)} custom-call(s32[7]{0:T(128)S(1)} %stack.41.scalars, bf16[64,1024]{1,0:T(8,128)(2,1)S(1)} %get-tuple-element.32.q_ref, bf16[128,256]{1,0:T(8,128)(2,1)S(1)} %pad_maximum_fusion.6.s0_ref, bf16[128,256]{1,0:T(8,128)(2,1)S(1)} %collective-permute-done.s1_ref, ...), custom_call_target="tpu_custom_call" | custom-call | flops 4563402752 | bytes 4194304 | tf_op jit(solution)/shard_map/attend/pallas_call | solution.py:128
  105.1 7.6 %collective-permute-start.16 = (bf16[64,1024]{1,0:T(8,128)(2,1)S(1)}, bf16[64,1024]{1,0:T(8,128)(2,1)S(1)}, u32[]{:S(2)}, u32[]{:S(2)}) collective-permute-start(bf16[64,1024]{1,0:T(8,128)(2,1)S(1)} %attend.11.refs_0_), channel_id=1, source_target_pairs={{0,4},{4,0},{8,12},{12,8},{16,20},{20,16},{24,28},{28,24},{32,36},... | collective-permute-start | bytes 393224 | tf_op jit(solution)/shard_map/ppermute | solution.py:272
  112.7 7.6 %project.6 = bf16[256,4096]{1,0:T(8,128)(2,1)S(1)} custom-call(bf16[128,1024]{1,0:T(8,128)(2,1)S(1)} %attend.6.refs_0_, bf16[128,1024]{1,0:T(8,128)(2,1)S(1)} %collective-permute-done.3.refs_1_, bf16[16,1024,256]{2,1,0:T(8,128)(2,1)} %bitcast.47), custom_call_target="tpu_custom_call" | custom-call | flops 2147483648 | bytes 8388608 | tf_op jit(solution)/shard_map/project/pallas_call | solution.py:191
  120.4 0.1 collective-permute-start.11
  120.5 0.1 fusion.3
  120.6 7.8 %project.10 = bf16[128,4096]{1,0:T(8,128)(2,1)S(1)} custom-call(bf16[64,1024]{1,0:T(8,128)(2,1)S(1)} %attend.10.refs_0_, bf16[64,1024]{1,0:T(8,128)(2,1)S(1)} %collective-permute-done.14.refs_1_, bf16[16,1024,256]{2,1,0:T(8,128)(2,1)} %bitcast.48, bf16[128,2048]{1,0:T(8,128)(2,1)S(1)} %pad_maximum_fusion.4.refs_3_), custom_call_target="tpu_custom_call" | custom-call | flops 1073741824 | bytes 8388608 | tf_op jit(solution)/shard_map/project/pallas_call | solution.py:191
  128.4 1.5 collective-permute-start.15
  129.9 0.1 fusion.4
  130.1 7.7 %project.11 = bf16[128,4096]{1,0:T(8,128)(2,1)S(1)} custom-call(bf16[64,1024]{1,0:T(8,128)(2,1)S(1)} %attend.11.refs_0_, bf16[64,1024]{1,0:T(8,128)(2,1)S(1)} %collective-permute-done.16.refs_1_, bf16[16,1024,256]{2,1,0:T(8,128)(2,1)} %bitcast.49, bf16[128,2048]{1,0:T(8,128)(2,1)S(1)} %pad_maximum_fusion.5.refs_3_), custom_call_target="tpu_custom_call" | custom-call | flops 1073741824 | bytes 8388608 | tf_op jit(solution)/shard_map/project/pallas_call | solution.py:191
  137.9 0.1 collective-permute-start.17
  138.0 0.2 fusion
  138.2 7.8 %project.8 = bf16[128,4096]{1,0:T(8,128)(2,1)S(1)} custom-call(bf16[64,1024]{1,0:T(8,128)(2,1)S(1)} %attend.7.refs_0_, bf16[64,1024]{1,0:T(8,128)(2,1)S(1)} %collective-permute-done.5.refs_1_, bf16[16,1024,256]{2,1,0:T(8,128)(2,1)} %bitcast.50, bf16[128,2048]{1,0:T(8,128)(2,1)S(1)} %pad_maximum_fusion.2.refs_3_), custom_call_target="tpu_custom_call" | custom-call | flops 1073741824 | bytes 8388608 | tf_op jit(solution)/shard_map/project/pallas_call | solution.py:191
  146.0 2.7 %collective-permute-start.9 = (bf16[128,4096]{1,0:T(8,128)(2,1)S(1)}, bf16[128,4096]{1,0:T(8,128)(2,1)S(1)}, u32[]{:S(2)}, u32[]{:S(2)}) collective-permute-start(bf16[128,4096]{1,0:T(8,128)(2,1)S(1)} %project.8), channel_id=1, source_target_pairs={{0,1},{1,2},{2,3},{3,0},{4,5},{5,6},{6,7},{7,4},{8,9},{9,10},{10,1... | collective-permute-start | bytes 3145736 | tf_op jit(solution)/shard_map/ppermute | solution.py:269
  148.8 7.7 %project.9 = bf16[128,4096]{1,0:T(8,128)(2,1)S(1)} custom-call(bf16[64,1024]{1,0:T(8,128)(2,1)S(1)} %attend.9.refs_0_, bf16[64,1024]{1,0:T(8,128)(2,1)S(1)} %collective-permute-done.11.refs_1_, bf16[16,1024,256]{2,1,0:T(8,128)(2,1)} %bitcast.51, bf16[128,2048]{1,0:T(8,128)(2,1)S(1)} %pad_maximum_fusion.3.refs_3_), custom_call_target="tpu_custom_call" | custom-call | flops 1073741824 | bytes 8388608 | tf_op jit(solution)/shard_map/project/pallas_call | solution.py:191
  156.5 0.1 collective-permute-start.13
  156.6 6.5 %collective-permute-done.17 = bf16[128,4096]{1,0:T(8,128)(2,1)S(1)} collective-permute-done((bf16[128,4096]{1,0:T(8,128)(2,1)S(1)}, bf16[128,4096]{1,0:T(8,128)(2,1)S(1)}, u32[]{:S(2)}, u32[]{:S(2)}) %collective-permute-start.17) | collective-permute-done | bytes 1048608 | tf_op jit(solution)/shard_map/ppermute | solution.py:269
  163.1 0.5 add_convert_fusion
  163.6 0.1 fusion.2
  163.7 11.5 %collective-permute-done.9 = bf16[128,4096]{1,0:T(8,128)(2,1)S(1)} collective-permute-done((bf16[128,4096]{1,0:T(8,128)(2,1)S(1)}, bf16[128,4096]{1,0:T(8,128)(2,1)S(1)}, u32[]{:S(2)}, u32[]{:S(2)}) %collective-permute-start.9) | collective-permute-done | bytes 1048608 | tf_op jit(solution)/shard_map/ppermute | solution.py:269
  175.2 10.4 %collective-permute-done.13 = bf16[128,4096]{1,0:T(8,128)(2,1)S(1)} collective-permute-done((bf16[128,4096]{1,0:T(8,128)(2,1)S(1)}, bf16[128,4096]{1,0:T(8,128)(2,1)S(1)}, u32[]{:S(2)}, u32[]{:S(2)}) %collective-permute-start.13) | collective-permute-done | bytes 1048608 | tf_op jit(solution)/shard_map/ppermute | solution.py:269
  185.6 0.5 add_convert_fusion.1
  186.0 0.1 fusion.1
  186.1 0.1 pad_maximum_fusion.1
  186.2 1.7 collective-permute-start.18
  187.9 0.8 pad_add_fusion.scalars
  188.7 0.1 pad_maximum_fusion.even_ref
  188.8 1.4 collective-permute-done.18.odd_ref
  190.2 2.6 %combine.1 = bf16[1,128,8192]{2,1,0:T(8,128)(2,1)} custom-call(s32[3]{0:T(128)S(1)} %pad_add_fusion.scalars, bf16[128,4096]{1,0:T(8,128)(2,1)S(1)} %pad_maximum_fusion.even_ref, bf16[128,4096]{1,0:T(8,128)(2,1)S(1)} %collective-permute-done.18.odd_ref), custom_call_target="tpu_custom_call" | custom-call | tf_op jit(solution)/shard_map/combine/pallas_call | solution.py:233
  (34 shorter events, 0.3 us)
Async XLA Ops:
  6.5 5.8 %copy-start.4 = (bf16[1,128,4096]{2,1,0:T(8,128)(2,1)S(1)}, bf16[1,128,4096]{2,1,0:T(8,128)(2,1)}, u32[]{:S(2)}) copy-start(bf16[1,128,4096]{2,1,0:T(8,128)(2,1)} %param.8) | copy-start | bytes 3145732
  6.5 8.6 %copy-start.5 = (s32[32]{0:T(128)S(1)}, s32[32]{0:T(128)}, u32[]{:S(2)}) copy-start(s32[32]{0:T(128)} %param.15) | copy-start | bytes 388
  6.5 9.2 %copy-start.6 = (s32[32]{0:T(128)S(1)}, s32[32]{0:T(128)}, u32[]{:S(2)}) copy-start(s32[32]{0:T(128)} %param.14) | copy-start | bytes 388
  6.5 75.9 %all-gather.3.cloned.1.call-start = ((), (), s32[]{:S(2)}) async-start(), calls=%async_computation | async-start | bytes 8912896 | tf_op jit(solution)/shard_map/all_gather | solution.py:266
  8.3 16.6 %collective-permute-start.1 = (bf16[128,256]{1,0:T(8,128)(2,1)S(1)}, bf16[128,256]{1,0:T(8,128)(2,1)S(1)}, u32[]{:S(2)}, u32[]{:S(2)}) collective-permute-start(bf16[128,256]{1,0:T(8,128)(2,1)S(1)} %pad_maximum_fusion.8), channel_id=1, source_target_pairs={{0,2},{1,3},{2,0},{3,1},{4,6},{5,7},{6,4},{7,5},{8,10},{9,11},{10,... | collective-permute-start | bytes 196616 | tf_op jit(solution)/shard_map/ppermute | solution.py:269
  9.5 15.5 %collective-permute-start = (bf16[128,256]{1,0:T(8,128)(2,1)S(1)}, bf16[128,256]{1,0:T(8,128)(2,1)S(1)}, u32[]{:S(2)}, u32[]{:S(2)}) collective-permute-start(bf16[128,256]{1,0:T(8,128)(2,1)S(1)} %pad_maximum_fusion.7), channel_id=1, source_target_pairs={{0,3},{1,0},{2,1},{3,2},{4,7},{5,4},{6,5},{7,6},{8,11},{9,8},{10,9... | collective-permute-start | bytes 196616 | tf_op jit(solution)/shard_map/ppermute | solution.py:269
  9.6 15.4 %collective-permute-start.2 = (bf16[128,256]{1,0:T(8,128)(2,1)S(1)}, bf16[128,256]{1,0:T(8,128)(2,1)S(1)}, u32[]{:S(2)}, u32[]{:S(2)}) collective-permute-start(bf16[128,256]{1,0:T(8,128)(2,1)S(1)} %pad_maximum_fusion.9), channel_id=1, source_target_pairs={{0,1},{1,2},{2,3},{3,0},{4,5},{5,6},{6,7},{7,4},{8,9},{9,10},{10,1... | collective-permute-start | bytes 196616 | tf_op jit(solution)/shard_map/ppermute | solution.py:269
  12.4 31.9 %collective-permute-start.4 = (bf16[128,1024]{1,0:T(8,128)(2,1)S(1)}, bf16[128,1024]{1,0:T(8,128)(2,1)S(1)}, u32[]{:S(2)}, u32[]{:S(2)}) collective-permute-start(bf16[128,1024]{1,0:T(8,128)(2,1)S(1)} %get-tuple-element.26), channel_id=1, source_target_pairs={{0,3},{1,0},{2,1},{3,2},{4,7},{5,4},{6,5},{7,6},{8,11},{9,8},{10,9... | collective-permute-start | bytes 786440 | tf_op jit(solution)/shard_map/ppermute | solution.py:269
  12.5 60.8 %collective-permute-start.10 = (bf16[128,1024]{1,0:T(8,128)(2,1)S(1)}, bf16[128,1024]{1,0:T(8,128)(2,1)S(1)}, u32[]{:S(2)}, u32[]{:S(2)}) collective-permute-start(bf16[128,1024]{1,0:T(8,128)(2,1)S(1)} %get-tuple-element.27), channel_id=1, source_target_pairs={{0,1},{1,2},{2,3},{3,0},{4,5},{5,6},{6,7},{7,4},{8,9},{9,10},{10,1... | collective-permute-start | bytes 786440 | tf_op jit(solution)/shard_map/ppermute | solution.py:269
  24.9 27.1 %collective-permute-start.6 = (bf16[128,1024]{1,0:T(8,128)(2,1)S(1)}, bf16[128,1024]{1,0:T(8,128)(2,1)S(1)}, u32[]{:S(2)}, u32[]{:S(2)}) collective-permute-start(bf16[128,1024]{1,0:T(8,128)(2,1)S(1)} %get-tuple-element.28), channel_id=1, source_target_pairs={{0,2},{1,3},{2,0},{3,1},{4,6},{5,7},{6,4},{7,5},{8,10},{9,11},{10,... | collective-permute-start | bytes 786440 | tf_op jit(solution)/shard_map/ppermute | solution.py:269
  25.0 1.6 copy-start
  26.6 1.6 copy-start.2
  42.2 63.0 %collective-permute-start.3 = (bf16[128,1024]{1,0:T(8,128)(2,1)S(1)}, bf16[128,1024]{1,0:T(8,128)(2,1)S(1)}, u32[]{:S(2)}, u32[]{:S(2)}) collective-permute-start(bf16[128,1024]{1,0:T(8,128)(2,1)S(1)} %attend.6.refs_0_), channel_id=1, source_target_pairs={{0,4},{4,0},{8,12},{12,8},{16,20},{20,16},{24,28},{28,24},{32,36},... | collective-permute-start | bytes 786440 | tf_op jit(solution)/shard_map/ppermute | solution.py:272
  49.0 71.6 %collective-permute-start.14 = (bf16[64,1024]{1,0:T(8,128)(2,1)S(1)}, bf16[64,1024]{1,0:T(8,128)(2,1)S(1)}, u32[]{:S(2)}, u32[]{:S(2)}) collective-permute-start(bf16[64,1024]{1,0:T(8,128)(2,1)S(1)} %attend.10.refs_0_), channel_id=1, source_target_pairs={{0,4},{4,0},{8,12},{12,8},{16,20},{20,16},{24,28},{28,24},{32,36},... | collective-permute-start | bytes 393224 | tf_op jit(solution)/shard_map/ppermute | solution.py:272
  60.3 12.9 %collective-permute-start.7 = (bf16[128,1024]{1,0:T(8,128)(2,1)S(1)}, bf16[128,1024]{1,0:T(8,128)(2,1)S(1)}, u32[]{:S(2)}, u32[]{:S(2)}) collective-permute-start(bf16[128,1024]{1,0:T(8,128)(2,1)S(1)} %attend.8.refs_0_), channel_id=1, source_target_pairs={{0,4},{4,0},{8,12},{12,8},{16,20},{20,16},{24,28},{28,24},{32,36},... | collective-permute-start | bytes 786440 | tf_op jit(solution)/shard_map/ppermute | solution.py:272
  70.3 67.9 %collective-permute-start.5 = (bf16[64,1024]{1,0:T(8,128)(2,1)S(1)}, bf16[64,1024]{1,0:T(8,128)(2,1)S(1)}, u32[]{:S(2)}, u32[]{:S(2)}) collective-permute-start(bf16[64,1024]{1,0:T(8,128)(2,1)S(1)} %attend.7.refs_0_), channel_id=1, source_target_pairs={{0,4},{4,0},{8,12},{12,8},{16,20},{20,16},{24,28},{28,24},{32,36},... | collective-permute-start | bytes 393224 | tf_op jit(solution)/shard_map/ppermute | solution.py:272
  82.4 11.4 %copy-start.1 = (bf16[1,1,8192,128]{3,2,1,0:T(8,128)(2,1)S(1)}, bf16[1,1,8192,128]{3,2,1,0:T(8,128)(2,1)}, u32[]{:S(2)}) copy-start(bf16[1,1,8192,128]{3,2,1,0:T(8,128)(2,1)} %param.11) | copy-start | bytes 6291460
  82.4 11.4 %copy-start.3 = (bf16[1,1,8192,128]{3,2,1,0:T(8,128)(2,1)S(1)}, bf16[1,1,8192,128]{3,2,1,0:T(8,128)(2,1)}, u32[]{:S(2)}) copy-start(bf16[1,1,8192,128]{3,2,1,0:T(8,128)(2,1)} %param.12) | copy-start | bytes 6291460
  93.5 26.9 %collective-permute-start.8 = (bf16[256,2048]{1,0:T(8,128)(2,1)S(1)}, bf16[256,2048]{1,0:T(8,128)(2,1)S(1)}, u32[]{:S(2)}, u32[]{:S(2)}) collective-permute-start(bf16[256,2048]{1,0:T(8,128)(2,1)S(1)} %get-tuple-element.7), channel_id=1, source_target_pairs={{0,1},{1,2},{2,3},{3,0},{4,5},{5,6},{6,7},{7,4},{8,9},{9,10},{10,1... | collective-permute-start | bytes 3145736 | tf_op jit(solution)/shard_map/ppermute | solution.py:269
  98.7 31.2 %collective-permute-start.12 = (bf16[256,2048]{1,0:T(8,128)(2,1)S(1)}, bf16[256,2048]{1,0:T(8,128)(2,1)S(1)}, u32[]{:S(2)}, u32[]{:S(2)}) collective-permute-start(bf16[256,2048]{1,0:T(8,128)(2,1)S(1)} %get-tuple-element.8), channel_id=1, source_target_pairs={{0,3},{1,0},{2,1},{3,2},{4,7},{5,4},{6,5},{7,6},{8,11},{9,8},{10,9... | collective-permute-start | bytes 3145736 | tf_op jit(solution)/shard_map/ppermute | solution.py:269
  105.1 25.0 %collective-permute-start.16 = (bf16[64,1024]{1,0:T(8,128)(2,1)S(1)}, bf16[64,1024]{1,0:T(8,128)(2,1)S(1)}, u32[]{:S(2)}, u32[]{:S(2)}) collective-permute-start(bf16[64,1024]{1,0:T(8,128)(2,1)S(1)} %attend.11.refs_0_), channel_id=1, source_target_pairs={{0,4},{4,0},{8,12},{12,8},{16,20},{20,16},{24,28},{28,24},{32,36},... | collective-permute-start | bytes 393224 | tf_op jit(solution)/shard_map/ppermute | solution.py:272
  120.4 28.4 %collective-permute-start.11 = (bf16[64,1024]{1,0:T(8,128)(2,1)S(1)}, bf16[64,1024]{1,0:T(8,128)(2,1)S(1)}, u32[]{:S(2)}, u32[]{:S(2)}) collective-permute-start(bf16[64,1024]{1,0:T(8,128)(2,1)S(1)} %attend.9.refs_0_), channel_id=1, source_target_pairs={{0,4},{4,0},{8,12},{12,8},{16,20},{20,16},{24,28},{28,24},{32,36},... | collective-permute-start | bytes 393224 | tf_op jit(solution)/shard_map/ppermute | solution.py:272
  128.4 28.2 %collective-permute-start.15 = (bf16[128,4096]{1,0:T(8,128)(2,1)S(1)}, bf16[128,4096]{1,0:T(8,128)(2,1)S(1)}, u32[]{:S(2)}, u32[]{:S(2)}) collective-permute-start(bf16[128,4096]{1,0:T(8,128)(2,1)S(1)} %project.10), channel_id=1, source_target_pairs={{0,1},{1,2},{2,3},{3,0},{4,5},{5,6},{6,7},{7,4},{8,9},{9,10},{10,1... | collective-permute-start | bytes 3145736 | tf_op jit(solution)/shard_map/ppermute | solution.py:269
  137.9 25.2 %collective-permute-start.17 = (bf16[128,4096]{1,0:T(8,128)(2,1)S(1)}, bf16[128,4096]{1,0:T(8,128)(2,1)S(1)}, u32[]{:S(2)}, u32[]{:S(2)}) collective-permute-start(bf16[128,4096]{1,0:T(8,128)(2,1)S(1)} %project.11), channel_id=1, source_target_pairs={{0,3},{1,0},{2,1},{3,2},{4,7},{5,4},{6,5},{7,6},{8,11},{9,8},{10,9... | collective-permute-start | bytes 3145736 | tf_op jit(solution)/shard_map/ppermute | solution.py:269
  146.0 29.2 %collective-permute-start.9 = (bf16[128,4096]{1,0:T(8,128)(2,1)S(1)}, bf16[128,4096]{1,0:T(8,128)(2,1)S(1)}, u32[]{:S(2)}, u32[]{:S(2)}) collective-permute-start(bf16[128,4096]{1,0:T(8,128)(2,1)S(1)} %project.8), channel_id=1, source_target_pairs={{0,1},{1,2},{2,3},{3,0},{4,5},{5,6},{6,7},{7,4},{8,9},{9,10},{10,1... | collective-permute-start | bytes 3145736 | tf_op jit(solution)/shard_map/ppermute | solution.py:269
  156.5 29.0 %collective-permute-start.13 = (bf16[128,4096]{1,0:T(8,128)(2,1)S(1)}, bf16[128,4096]{1,0:T(8,128)(2,1)S(1)}, u32[]{:S(2)}, u32[]{:S(2)}) collective-permute-start(bf16[128,4096]{1,0:T(8,128)(2,1)S(1)} %project.9), channel_id=1, source_target_pairs={{0,3},{1,0},{2,1},{3,2},{4,7},{5,4},{6,5},{7,6},{8,11},{9,8},{10,9... | collective-permute-start | bytes 3145736 | tf_op jit(solution)/shard_map/ppermute | solution.py:269
  186.2 4.0 %collective-permute-start.18 = (bf16[128,4096]{1,0:T(8,128)(2,1)S(1)}, bf16[128,4096]{1,0:T(8,128)(2,1)S(1)}, u32[]{:S(2)}, u32[]{:S(2)}) collective-permute-start(bf16[128,4096]{1,0:T(8,128)(2,1)S(1)} %pad_maximum_fusion.1), channel_id=1, source_target_pairs={{0,4},{4,0},{8,12},{12,8},{16,20},{20,16},{24,28},{28,24},{32,36},... | collective-permute-start | bytes 3145736 | tf_op jit(solution)/shard_map/ppermute | solution.py:272
Sparse Core Ops, SparseCore 0:
  9.5 72.8 all-gather.2
